TPU v7x, 32 devices: a whole 2x2x4 slice. The times are simulated.
32 devices in a mesh: section: 4 (over y, x), expert: 8 (over z, core).
Axes of the slice: x: 2, y: 2, z: 4, core: 2. Of those that a mesh axis runs over, the one named last changes fastest.
Arguments:
- forward_input: bfloat16 [4, 576, 4096], P('section', 'expert'), may hold values from -6 to 6
- backward_cotangent: bfloat16 [4, 576, 4096], P('section', 'expert'), may hold values from -6 to 6
- saved_input: bfloat16 [4, 576, 4096], P('section', 'expert'), may hold values from -6 to 6
- saved_hidden: bfloat16 [4, 8, 360, 1536], P('section', 'expert'), may hold values from -8 to 8
- norm_gain: float32 [4, 4096], P('section'), may hold values from 0.5 to 2
- forward_experts: int32 [4, 576, 4], P('section', 'expert'), may hold values from 0 to 7, all different within a row; in each aligned block of 72 rows (0 to 71, 72 to 143, ..., all dimensions but the last counted through in order) at most 45 rows name the same one
- forward_gates: float32 [4, 576, 4], P('section', 'expert'), may hold values from 0.05 to 1
- backward_experts: int32 [4, 576, 4], P('section', 'expert'), may hold values from 0 to 7, all different within a row; in each aligned block of 72 rows (0 to 71, 72 to 143, ..., all dimensions but the last counted through in order) at most 45 rows name the same one
- backward_gates: float32 [4, 576, 4], P('section', 'expert'), may hold values from 0.05 to 1
- gate_up_weight: bfloat16 [4, 8, 4096, 1536], P('section', 'expert'), may hold values from -0.09375 to 0.09375
- down_weight: bfloat16 [4, 8, 768, 4096], P('section', 'expert'), may hold values from -0.21875 to 0.21875
Outputs:
- forward_output: bfloat16 [4, 576, 4096], P('section', 'expert')
- input_gradient: bfloat16 [4, 576, 4096], P('section', 'expert')
Inputs may be any that keep to these rules, and one draw needn't show every extreme that they name: `forward_experts`: each token names 4 distinct experts. In the rows of one device (aligned blocks of 72 tokens) no expert is named by more than 45 entries, and in some device's rows some expert is named by exactly 45. `backward_experts`: same law as forward_experts, drawn independently.
All inputs are finite; a program needn't handle non-finite values.
Results may differ from a plain program's by a relative error of at most 0.0054.
Values may be sent and summed in bfloat16 or wider, within the bound.
A program may use at most 128 MiB of HBM per device.

v0:
```python
import jax
import jax.numpy as jnp
from jax import lax
from jax.sharding import PartitionSpec as P

EPSILON = 1e-06


def passed_along(value, axis, steps):
    count = lax.axis_size(axis)
    initial, last = (max(0, -steps), min(count, count - steps))
    return lax.ppermute(value, axis, [(source, source + steps) for source in range(initial, last)])


def norm_scale(values, gain_row):
    widened = values.astype(jnp.float32)
    inverse = lax.rsqrt(jnp.mean(widened * widened, axis=-1, keepdims=True) + EPSILON)
    return widened * inverse * gain_row


def normalized(gate_values):
    return gate_values / jnp.sum(gate_values, axis=-1, keepdims=True)


def block_slots(expert_ids, peer_count):
    flat_ids = expert_ids.reshape(-1)
    onehot = (flat_ids[:, None] == jnp.arange(peer_count, dtype=jnp.int32)[None, :]).astype(
        jnp.int32
    )
    rank_table = jnp.cumsum(onehot, axis=0) - 1
    slot_index = jnp.sum(rank_table * onehot, axis=1)
    return (flat_ids, slot_index)


def local_rows(expert_ids, peer_count, capacity):
    flat_ids, slot_index = block_slots(expert_ids, peer_count)
    return flat_ids * capacity + slot_index


def expert_forward(inputs, weight_in, weight_down):
    hidden_width = weight_down.shape[0]
    projected = jnp.dot(inputs, weight_in, preferred_element_type=jnp.float32)
    hidden = (jax.nn.silu(projected[:, :hidden_width]) * projected[:, hidden_width:]).astype(
        jnp.bfloat16
    )
    return jnp.dot(hidden, weight_down, preferred_element_type=jnp.float32).astype(jnp.bfloat16)


def expert_backward(cotangent_rows, saved_rows, weight_in, weight_down):
    hidden_width = weight_down.shape[0]
    grad_hidden = lax.dot_general(
        cotangent_rows, weight_down, (((1,), (1,)), ((), ())), preferred_element_type=jnp.float32
    )
    gate_value = saved_rows[:, :hidden_width].astype(jnp.float32)
    upward = saved_rows[:, hidden_width:].astype(jnp.float32)
    sigmoid_gate = jax.nn.sigmoid(gate_value)
    grad_gate = grad_hidden * upward * sigmoid_gate * (1.0 + gate_value * (1.0 - sigmoid_gate))
    grad_upper = grad_hidden * gate_value * sigmoid_gate
    grad_both = jnp.concatenate([grad_gate, grad_upper], axis=1).astype(jnp.bfloat16)
    return lax.dot_general(
        grad_both, weight_in, (((1,), (1,)), ((), ())), preferred_element_type=jnp.float32
    ).astype(jnp.bfloat16)


def local(
    forward_input,
    backward_cotangent,
    saved_input,
    saved_hidden,
    norm_gain,
    forward_experts,
    forward_gates,
    backward_experts,
    backward_gates,
    gate_up_weight,
    down_weight,
):
    moved_input, moved_cotangent = passed_along((forward_input, backward_cotangent), "section", 1)
    is_first = lax.axis_index("section") == 0
    layer_in = jnp.where(is_first, forward_input, moved_input)[0]
    cotangent = jnp.where(is_first, backward_cotangent, moved_cotangent)[0]
    peer_count = lax.axis_size("expert")
    model_width = layer_in.shape[1]
    token_count = layer_in.shape[0]
    top_count = forward_experts.shape[2]
    slot_total = saved_hidden.shape[2]
    capacity = slot_total // peer_count
    gain_row = norm_gain[0]
    weight_in = gate_up_weight[0, 0]
    weight_down = down_weight[0, 0]
    saved_rows = saved_hidden[0, 0]
    normed = norm_scale(layer_in, gain_row).astype(jnp.bfloat16)
    forward_rows = local_rows(forward_experts[0], peer_count, capacity)
    backward_rows = local_rows(backward_experts[0], peer_count, capacity)
    empty = jnp.zeros((slot_total, model_width), jnp.bfloat16)
    send_forward = (
        empty.at[forward_rows]
        .set(jnp.repeat(normed, top_count, axis=0))
        .reshape(peer_count, capacity, model_width)
    )
    scaled = (
        normalized(backward_gates[0])[:, :, None] * cotangent.astype(jnp.float32)[:, None, :]
    ).astype(jnp.bfloat16)
    send_backward = (
        empty.at[backward_rows]
        .set(scaled.reshape(-1, model_width))
        .reshape(peer_count, capacity, model_width)
    )
    received = lax.all_to_all(send_forward, "expert", split_axis=0, concat_axis=0, tiled=True)
    count = received.shape[1]
    served_rows = expert_forward(received.reshape(-1, model_width), weight_in, weight_down).reshape(
        peer_count, count, model_width
    )
    back_forward = lax.all_to_all(served_rows, "expert", split_axis=0, concat_axis=0, tiled=True)
    arrived = lax.all_to_all(send_backward, "expert", split_axis=0, concat_axis=0, tiled=True)
    grads = expert_backward(
        arrived.reshape(-1, model_width), saved_rows, weight_in, weight_down
    ).reshape(peer_count, capacity, model_width)
    back_backward = lax.all_to_all(grads, "expert", split_axis=0, concat_axis=0, tiled=True)
    picked = back_forward.reshape(slot_total, model_width)[forward_rows].reshape(
        token_count, top_count, model_width
    )
    mixture = jnp.einsum("tk,tkd->td", normalized(forward_gates[0]), picked.astype(jnp.float32))
    forward_output = (layer_in.astype(jnp.float32) + mixture).astype(jnp.bfloat16)
    gathered = back_backward.reshape(slot_total, model_width)[backward_rows].reshape(
        token_count, top_count, model_width
    )
    grad_normed = jnp.sum(gathered.astype(jnp.float32), axis=1)

    def apply_norm(inputs):
        return norm_scale(inputs, gain_row)

    primal, pullback = jax.vjp(apply_norm, saved_input[0].astype(jnp.float32))
    input_gradient = (cotangent.astype(jnp.float32) + pullback(grad_normed)[0]).astype(jnp.bfloat16)
    return (forward_output[None], input_gradient[None])


def solution(mesh):
    in_specs = (
        P("section", "expert", None),
        P("section", "expert", None),
        P("section", "expert", None),
        P("section", "expert", None, None),
        P("section", None),
        P("section", "expert", None),
        P("section", "expert", None),
        P("section", "expert", None),
        P("section", "expert", None),
        P("section", "expert", None, None),
        P("section", "expert", None, None),
    )
    out_specs = (P("section", "expert", None), P("section", "expert", None))
    return jax.shard_map(local, mesh=mesh, in_specs=in_specs, out_specs=out_specs, check_vma=False)
```

profile of v0, /device:TPU:0, one launch (start us, length us, event | category | flops | bytes accessed | tf_op | source)
XLA Modules:
  0.0 432.2 jit_solution(11699666504679697321)
XLA Ops:
  0.6 4.9 %collective-permute-start.1 = (bf16[1,72,4096]{2,1,0:T(8,128)(2,1)}, bf16[1,72,4096]{2,1,0:T(8,128)(2,1)S(1)}, u32[]{:S(2)}, u32[]{:S(2)}) collective-permute-start(bf16[1,72,4096]{2,1,0:T(8,128)(2,1)} %param.12), channel_id=1, source_target_pairs={{0,8},{8,16},{16,24},{1,9},{9,17},{17,25},{2,10},{10,18},{18,26},{... | collective-permute-start | bytes 1769480 | tf_op jit(solution)/shard_map/ppermute | solution.py:12
  5.5 0.8 copy.16
  6.3 0.1 eq.55
  6.4 0.9 reduce-window.16
  7.3 0.2 slice_reduce_fusion
  7.5 0.7 broadcast_multiply_fusion
  8.2 0.1 copy.15
  8.3 0.1 mul.164
  8.5 0.8 copy.17
  9.2 0.7 reduce_sum.88
  9.9 0.1 div.48
  10.0 0.1 div.49
  10.1 0.1 squeeze.21
  10.2 0.1 add_bitcast_fusion
  10.4 8.0 %collective-permute-done.1 = bf16[1,72,4096]{2,1,0:T(8,128)(2,1)S(1)} collective-permute-done((bf16[1,72,4096]{2,1,0:T(8,128)(2,1)}, bf16[1,72,4096]{2,1,0:T(8,128)(2,1)S(1)}, u32[]{:S(2)}, u32[]{:S(2)}) %collective-permute-start.1) | collective-permute-done | bytes 589856 | tf_op jit(solution)/shard_map/ppermute | solution.py:12
  18.4 1.4 convert_bitcast_fusion.1
  19.7 3.5 mul.167
  23.2 6.4 %mul.168 = f32[288,4096]{1,0:T(8,128)} reshape(f32[72,4,4096]{2,1,0:T(4,128)} %mul.167) | data formatting | bytes 9437184 | tf_op jit(solution)/shard_map/mul | solution.py:102
  29.6 7.6 %scatter_custom_fusion.1 = bf16[360,4096]{1,0:T(8,128)(2,1)} fusion(s32[288]{0:T(512)S(1)} %fusion.50, f32[288,4096]{1,0:T(8,128)} %mul.168, f32[288]{0:T(512)S(1)} %div.50, bf16[]{:T(256)} %constant.32.clone.1), kind=kCustom, calls=%fused_computation.15 | custom fusion | flops 2359296 | bytes 7669762 | tf_op jit(solution)/shard_map/scatter | solution.py:106
  37.2 2.7 reshape.241
  39.9 76.8 %all_to_all.20 = bf16[8,45,4096]{2,1,0:T(8,128)(2,1)} all-to-all(bf16[8,45,4096]{2,1,0:T(8,128)(2,1)S(1)} %reshape.241), channel_id=1, replica_groups=mesh['section'=4,'expert'=8] {'expert'}, dimensions={0} | all-to-all | bytes 5898240 | tf_op jit(solution)/shard_map/all_to_all | solution.py:115
  116.8 2.8 reshape.242
  119.6 5.8 %fusion.34 = (bf16[360,768]{1,0:T(8,128)(2,1)S(1)}, bf16[360,768]{1,0:T(8,128)(2,1)S(1)}) fusion(bf16[360,1536]{1,0:T(8,128)(2,1)} %bitcast.75, bf16[360,4096]{1,0:T(8,128)(2,1)S(1)} %reshape.242, bf16[1,1,768,4096]{3,2,1,0:T(8,128)(2,1)} %param.21), kind=kOutput, calls=%fused_computation.47 | convolution fusion | flops 2269071360 | bytes 11452416 | tf_op jit(solution)/shard_map/dot_general | solution.py:51
  125.4 13.0 %fusion.11 = bf16[360,4096]{1,0:T(8,128)(2,1)S(1)} fusion(bf16[1,1,4096,1536]{3,2,1,0:T(8,128)(2,1)} %param.20, bf16[360,768]{1,0:T(8,128)(2,1)S(1)} %get-tuple-element.7, bf16[360,768]{1,0:T(8,128)(2,1)S(1)} %get-tuple-element.6), kind=kOutput, calls=%fused_computation.13 | convolution fusion | flops 4533534720 | bytes 16637952 | tf_op jit(solution)/shard_map/dot_general | solution.py:60
  138.4 2.6 reshape.243
  141.0 4.6 %all-to-all-start.3 = ((bf16[8,45,4096]{2,1,0:T(8,128)(2,1)}), bf16[8,45,4096]{2,1,0:T(8,128)(2,1)}, u32[]{:S(2)}, u32[]{:S(2)}) async-start(bf16[8,45,4096]{2,1,0:T(8,128)(2,1)} %reshape.243), calls=%async_computation.3 | async-start | bytes 6291456 | tf_op jit(solution)/shard_map/all_to_all | solution.py:119
  145.6 3.2 collective-permute-start
  148.8 0.1 copy.14
  148.9 0.1 eq.48
  149.1 0.9 reduce-window.14
  149.9 0.2 slice_reduce_fusion.1
  150.2 0.1 copy.13
  150.3 0.1 mul.153
  150.4 0.1 add_bitcast_fusion.1
  150.5 0.6 fusion.49
  151.1 10.6 %collective-permute-done = bf16[1,72,4096]{2,1,0:T(8,128)(2,1)S(1)} collective-permute-done((bf16[1,72,4096]{2,1,0:T(8,128)(2,1)S(1)}, bf16[1,72,4096]{2,1,0:T(8,128)(2,1)S(1)}, u32[]{:S(2)}, u32[]{:S(2)}) %collective-permute-start) | collective-permute-done | bytes 589856 | tf_op jit(solution)/shard_map/ppermute | solution.py:12
  161.7 0.3 fusion.24
  162.0 0.5 add_rsqrt_fusion
  162.6 54.6 %all-to-all-done.3 = bf16[8,45,4096]{2,1,0:T(8,128)(2,1)} async-done(((bf16[8,45,4096]{2,1,0:T(8,128)(2,1)}), bf16[8,45,4096]{2,1,0:T(8,128)(2,1)}, u32[]{:S(2)}, u32[]{:S(2)}) %all-to-all-start.3) | async-done | bytes 2949152 | tf_op jit(solution)/shard_map/all_to_all | solution.py:119
  217.1 2.8 reshape.244
  219.9 3.8 gather_fusion.1
  223.7 5.5 %reshape.249 = f32[72,4,4096]{2,1,0:T(4,128)} reshape(bf16[288,4096]{1,0:T(8,128)(2,1)} %gather_fusion.1) | data formatting | bytes 7077888 | tf_op jit(solution)/shard_map/convert_element_type | solution.py:128
  229.2 5.3 %reduce_sum.89 = f32[72,4096]{1,0:T(8,128)S(1)} reduce(f32[72,4,4096]{2,1,0:T(4,128)} %reshape.249, f32[]{:T(128)} %constant.31.clone.1), dimensions={1}, to_apply=%region_11.12 | reduce | flops 884736 | bytes 5898244 | tf_op jit(solution)/shard_map/reduce_sum | solution.py:128
  234.6 1.0 fusion.22
  235.6 1.1 broadcast_in_dim.9
  236.7 2.1 reshape.271
  238.9 7.0 %scatter_custom_fusion = bf16[360,4096]{1,0:T(8,128)(2,1)} fusion(s32[288]{0:T(512)} %fusion.49, bf16[288,4096]{1,0:T(8,128)(2,1)} %reshape.271, bf16[]{:T(256)} %constant.32.clone.1), kind=kCustom, calls=%fused_computation.31 | custom fusion | bytes 2949632 | tf_op jit(solution)/shard_map/scatter | solution.py:98
  245.9 2.7 reshape.234
  248.6 74.7 %all_to_all.21 = bf16[8,45,4096]{2,1,0:T(8,128)(2,1)} all-to-all(bf16[8,45,4096]{2,1,0:T(8,128)(2,1)S(1)} %reshape.234), channel_id=1, replica_groups=mesh['section'=4,'expert'=8] {'expert'}, dimensions={0} | all-to-all | bytes 5898240 | tf_op jit(solution)/shard_map/all_to_all | solution.py:109
  323.4 2.8 reshape.235
  326.2 7.7 %fusion.2 = f32[360,1536]{1,0:T(8,128)S(1)} fusion(bf16[360,4096]{1,0:T(8,128)(2,1)S(1)} %reshape.235, bf16[1,1,4096,1536]{3,2,1,0:T(8,128)(2,1)} %param.20), kind=kOutput, calls=%fused_computation.6 | convolution fusion | flops 4529848320 | bytes 17743872 | tf_op jit(solution)/shard_map/dot_general | solution.py:42
  333.9 5.3 %fusion.8 = bf16[360,4096]{1,0:T(8,128)(2,1)S(1)} fusion(bf16[1,1,768,4096]{3,2,1,0:T(8,128)(2,1)} %param.21, f32[360,1536]{1,0:T(8,128)S(1)} %fusion.2), kind=kOutput, calls=%fused_computation.12 | convolution fusion | flops 2268057600 | bytes 11452416 | tf_op jit(solution)/shard_map/dot_general | solution.py:46
  339.2 2.6 reshape.236
  341.9 0.0 copy-start.4
  341.9 0.0 copy-start.6
  341.9 5.0 %all-to-all-start.1 = ((bf16[8,45,4096]{2,1,0:T(8,128)(2,1)}), bf16[8,45,4096]{2,1,0:T(8,128)(2,1)}, u32[]{:S(2)}, u32[]{:S(2)}) async-start(bf16[8,45,4096]{2,1,0:T(8,128)(2,1)} %reshape.236), calls=%async_computation.1 | async-start | bytes 6291456 | tf_op jit(solution)/shard_map/all_to_all | solution.py:114
  346.9 0.1 copy.18
  347.1 1.2 fusion.21
  348.4 70.0 %all-to-all-done.1 = bf16[8,45,4096]{2,1,0:T(8,128)(2,1)} async-done(((bf16[8,45,4096]{2,1,0:T(8,128)(2,1)}), bf16[8,45,4096]{2,1,0:T(8,128)(2,1)}, u32[]{:S(2)}, u32[]{:S(2)}) %all-to-all-start.1) | async-done | bytes 2949152 | tf_op jit(solution)/shard_map/all_to_all | solution.py:114
  418.4 2.8 reshape.237
  421.2 3.8 gather_fusion
  425.0 4.1 reshape.238
  429.1 1.4 fusion.54
  430.5 1.5 fusion.41
  (48 shorter events, 0.3 us)
Async XLA Ops:
  0.6 17.7 %collective-permute-start.1 = (bf16[1,72,4096]{2,1,0:T(8,128)(2,1)}, bf16[1,72,4096]{2,1,0:T(8,128)(2,1)S(1)}, u32[]{:S(2)}, u32[]{:S(2)}) collective-permute-start(bf16[1,72,4096]{2,1,0:T(8,128)(2,1)} %param.12), channel_id=1, source_target_pairs={{0,8},{8,16},{16,24},{1,9},{9,17},{17,25},{2,10},{10,18},{18,26},{... | collective-permute-start | bytes 1769480 | tf_op jit(solution)/shard_map/ppermute | solution.py:12
  18.4 4.9 %copy-start.5 = (bf16[1,72,4096]{2,1,0:T(8,128)(2,1)}, bf16[1,72,4096]{2,1,0:T(8,128)(2,1)S(1)}, u32[]{:S(2)}) copy-start(bf16[1,72,4096]{2,1,0:T(8,128)(2,1)S(1)} %collective-permute-done.1) | copy-start | bytes 1769476
  141.0 4.6 %copy-start.9 = (bf16[1,72,4096]{2,1,0:T(8,128)(2,1)S(1)}, bf16[1,72,4096]{2,1,0:T(8,128)(2,1)}, u32[]{:S(2)}) copy-start(bf16[1,72,4096]{2,1,0:T(8,128)(2,1)} %param.11) | copy-start | bytes 1769476
  141.0 7.8 %copy-start.11 = (s32[1,72,4]{1,2,0:T(4,128)S(1)}, s32[1,72,4]{1,2,0:T(4,128)}, u32[]{:S(2)}) copy-start(s32[1,72,4]{1,2,0:T(4,128)} %param.16) | copy-start | bytes 3460
  141.0 76.1 %all-to-all-start.3 = ((bf16[8,45,4096]{2,1,0:T(8,128)(2,1)}), bf16[8,45,4096]{2,1,0:T(8,128)(2,1)}, u32[]{:S(2)}, u32[]{:S(2)}) async-start(bf16[8,45,4096]{2,1,0:T(8,128)(2,1)} %reshape.243), calls=%async_computation.3 | async-start | bytes 6291456 | tf_op jit(solution)/shard_map/all_to_all | solution.py:119
  145.6 16.1 %collective-permute-start = (bf16[1,72,4096]{2,1,0:T(8,128)(2,1)S(1)}, bf16[1,72,4096]{2,1,0:T(8,128)(2,1)S(1)}, u32[]{:S(2)}, u32[]{:S(2)}) collective-permute-start(bf16[1,72,4096]{2,1,0:T(8,128)(2,1)S(1)} %copy-done.9), channel_id=1, source_target_pairs={{0,8},{8,16},{16,24},{1,9},{9,17},{17,25},{2,10},{10,18},{18,26},{... | collective-permute-start | bytes 1769480 | tf_op jit(solution)/shard_map/ppermute | solution.py:12
  162.0 72.5 %copy-start.2 = (bf16[1,72,4096]{2,1,0:T(8,128)(2,1)}, bf16[1,72,4096]{2,1,0:T(8,128)(2,1)S(1)}, u32[]{:S(2)}) copy-start(bf16[1,72,4096]{2,1,0:T(8,128)(2,1)S(1)} %get-tuple-element.5) | copy-start | bytes 1769476
  229.2 5.4 %copy-start.7 = (bf16[1,72,4096]{2,1,0:T(8,128)(2,1)S(1)}, bf16[1,72,4096]{2,1,0:T(8,128)(2,1)}, u32[]{:S(2)}) copy-start(bf16[1,72,4096]{2,1,0:T(8,128)(2,1)} %param.13) | copy-start | bytes 1769476
  229.2 5.4 %copy-start.10 = (f32[1,4096]{1,0:T(1,128)S(1)}, f32[1,4096]{1,0:T(1,128)}, u32[]{:S(2)}) copy-start(f32[1,4096]{1,0:T(1,128)} %param.15) | copy-start | bytes 49156
  229.2 5.4 %copy-start.16 = (f32[72]{0:T(128)S(1)}, f32[72]{0:T(128)}, u32[]{:S(2)}) copy-start(f32[72]{0:T(128)} %add_rsqrt_fusion) | copy-start | bytes 868
  234.5 2.2 copy-start
  341.8 5.0 %copy-start.12 = (f32[1,72,4]{1,2,0:T(4,128)S(1)}, f32[1,72,4]{1,2,0:T(4,128)}, u32[]{:S(2)}) copy-start(f32[1,72,4]{1,2,0:T(4,128)} %param.17) | copy-start | bytes 3460
  341.9 5.2 %copy-start.13 = (s32[288]{0:T(512)S(1)}, s32[288]{0:T(512)}, u32[]{:S(2)}) copy-start(s32[288]{0:T(512)} %fusion.49) | copy-start | bytes 3460
  341.9 5.2 %copy-start.14 = (f32[72]{0:T(128)S(1)}, f32[72]{0:T(128)}, u32[]{:S(2)}) copy-start(f32[72]{0:T(128)} %get-tuple-element.2) | copy-start | bytes 868
  341.9 5.2 %copy-start.15 = (f32[72]{0:T(128)S(1)}, f32[72]{0:T(128)}, u32[]{:S(2)}) copy-start(f32[72]{0:T(128)} %get-tuple-element.3) | copy-start | bytes 868
  341.9 5.2 %copy-start.1 = (f32[72,4096]{1,0:T(8,128)S(1)}, f32[72,4096]{1,0:T(8,128)}, u32[]{:S(2)}) copy-start(f32[72,4096]{1,0:T(8,128)} %copy-done) | copy-start | bytes 3538948
  341.9 5.2 %copy-start.4 = (bf16[1,72,4096]{2,1,0:T(8,128)(2,1)S(1)}, bf16[1,72,4096]{2,1,0:T(8,128)(2,1)}, u32[]{:S(2)}) copy-start(bf16[1,72,4096]{2,1,0:T(8,128)(2,1)} %param.12) | copy-start | bytes 1769476
  341.9 5.2 %copy-start.6 = (bf16[1,72,4096]{2,1,0:T(8,128)(2,1)S(1)}, bf16[1,72,4096]{2,1,0:T(8,128)(2,1)}, u32[]{:S(2)}) copy-start(bf16[1,72,4096]{2,1,0:T(8,128)(2,1)} %copy-done.5) | copy-start | bytes 1769476
  341.9 5.2 %copy-start.8 = (bf16[1,72,4096]{2,1,0:T(8,128)(2,1)S(1)}, bf16[1,72,4096]{2,1,0:T(8,128)(2,1)}, u32[]{:S(2)}) copy-start(bf16[1,72,4096]{2,1,0:T(8,128)(2,1)} %param.13) | copy-start | bytes 1769476
  341.9 76.5 %all-to-all-start.1 = ((bf16[8,45,4096]{2,1,0:T(8,128)(2,1)}), bf16[8,45,4096]{2,1,0:T(8,128)(2,1)}, u32[]{:S(2)}, u32[]{:S(2)}) async-start(bf16[8,45,4096]{2,1,0:T(8,128)(2,1)} %reshape.236), calls=%async_computation.1 | async-start | bytes 6291456 | tf_op jit(solution)/shard_map/all_to_all | solution.py:114
  429.1 1.4 copy-start.3
where the time goes:
time: 439 us; the launch traced here: 432 us
  blocking collectives  152 us (35%)
  waiting for transfers between devices  143 us (33%)
  local copies, waits for them, and re-layouts  62.3 us (14%)
  matrix products  33.2 us (8%)
  other arithmetic  23 us (5%)
  starting transfers between devices  17.6 us (4%)
    all_to_all x1, blocking collectives, local(): lax.all_to_all(send_backward, 'expert', split_axis=0, concat_axis=0, tile...  76.8 us
    all_to_all x1, blocking collectives, local(): lax.all_to_all(send_forward, 'expert', split_axis=0, concat_axis=0, tiled...  74.7 us
    all_to_all x1, waiting for transfers between devices, local(): lax.all_to_all(served_rows, 'expert', split_axis=0, concat_axis=0, tiled=...  70 us
    all_to_all x1, waiting for transfers between devices, local(): lax.all_to_all(grads, 'expert', split_axis=0, concat_axis=0, tiled=True)  54.6 us
    ppermute x2, waiting for transfers between devices, passed_along(): lax.ppermute(value, axis, [(source, source + steps) for source in range(i...  18.6 us
    dot_general x1, matrix products, expert_backward(): lax.dot_general(grad_both, weight_in, (((1,), (1,)), ((), ())), preferred...  13 us
    mul x2, local copies, waits for them, and re-layouts, local(): normalized(backward_gates[0])[:, :, None]  9.87 us
  transfers between devices with their start and end apart: 4, of which 4 were waited for; matrix products, arithmetic and copies ran while one was open for 2% of the time, Pallas kernels for 0%

commit v1 on v0

v1 whole, which is shorter than its diff:
```python
import jax
import jax.numpy as jnp
from jax import lax
from jax.sharding import PartitionSpec as P

EPSILON = 1e-06


def passed_along(value, axis, steps):
    count = lax.axis_size(axis)
    initial, last = (max(0, -steps), min(count, count - steps))
    return lax.ppermute(value, axis, [(source, source + steps) for source in range(initial, last)])


def norm_scale(values, gain_row):
    widened = values.astype(jnp.float32)
    inverse = lax.rsqrt(jnp.mean(widened * widened, axis=-1, keepdims=True) + EPSILON)
    return widened * inverse * gain_row


def dense_weights(expert_ids, gates, expert_count):
    weights = gates / jnp.sum(gates, axis=-1, keepdims=True)
    onehot = expert_ids[:, :, None] == jnp.arange(expert_count, dtype=jnp.int32)[None, None, :]
    return jnp.sum(jnp.where(onehot, weights[:, :, None], 0.0), axis=1)


def local(
    forward_input,
    backward_cotangent,
    saved_input,
    saved_hidden,
    norm_gain,
    forward_experts,
    forward_gates,
    backward_experts,
    backward_gates,
    gate_up_weight,
    down_weight,
):
    peer_count = lax.axis_size("expert")
    me = lax.axis_index("expert")
    table = jnp.concatenate(
        [
            dense_weights(forward_experts[0], forward_gates[0], peer_count),
            dense_weights(backward_experts[0], backward_gates[0], peer_count),
        ],
        axis=1,
    )
    tables = lax.all_gather(table, "expert", axis=0, tiled=True)
    weight_f = lax.dynamic_slice_in_dim(tables, me, 1, axis=1)
    weight_b = lax.dynamic_slice_in_dim(tables, peer_count + me, 1, axis=1)

    moved_input, moved_cotangent = passed_along((forward_input, backward_cotangent), "section", 1)
    is_first = lax.axis_index("section") == 0
    layer_in = jnp.where(is_first, forward_input, moved_input)[0]
    cotangent = jnp.where(is_first, backward_cotangent, moved_cotangent)[0]
    token_count = layer_in.shape[0]
    slot_total = saved_hidden.shape[2]
    capacity = slot_total // peer_count
    gain_row = norm_gain[0]
    weight_in = gate_up_weight[0, 0]
    weight_down = down_weight[0, 0]
    hidden_width = weight_down.shape[0]

    normed = norm_scale(layer_in, gain_row).astype(jnp.bfloat16)
    all_normed = lax.all_gather(normed, "expert", axis=0, tiled=True)
    all_cotangent = lax.all_gather(cotangent, "expert", axis=0, tiled=True)

    projected = jnp.dot(all_normed, weight_in, preferred_element_type=jnp.float32)
    hidden = (jax.nn.silu(projected[:, :hidden_width]) * projected[:, hidden_width:]).astype(
        jnp.bfloat16
    )
    served = jnp.dot(hidden, weight_down, preferred_element_type=jnp.float32)
    served = (served * weight_f).astype(jnp.bfloat16)
    mixture = lax.psum_scatter(served, "expert", scatter_dimension=0, tiled=True)
    forward_output = (layer_in.astype(jnp.float32) + mixture.astype(jnp.float32)).astype(
        jnp.bfloat16
    )

    routed = (weight_b > 0.0).reshape(peer_count, token_count)
    slot = jnp.cumsum(routed.astype(jnp.int32), axis=1) - 1
    spread = (
        (slot[:, :, None] == jnp.arange(capacity, dtype=jnp.int32)[None, None, :])
        & routed[:, :, None]
    ).astype(jnp.bfloat16)
    saved = jnp.einsum(
        "jts,jsf->jtf",
        spread,
        saved_hidden[0, 0].reshape(peer_count, capacity, -1),
        preferred_element_type=jnp.float32,
    ).reshape(peer_count * token_count, -1)
    scaled = (weight_b * all_cotangent.astype(jnp.float32)).astype(jnp.bfloat16)
    grad_hidden = lax.dot_general(
        scaled, weight_down, (((1,), (1,)), ((), ())), preferred_element_type=jnp.float32
    )
    gate, up = saved[:, :hidden_width], saved[:, hidden_width:]
    sig = jax.nn.sigmoid(gate)
    grad_both = jnp.concatenate(
        [grad_hidden * up * sig * (1.0 + gate * (1.0 - sig)), grad_hidden * gate * sig], axis=1
    ).astype(jnp.bfloat16)
    grads = lax.dot_general(
        grad_both, weight_in, (((1,), (1,)), ((), ())), preferred_element_type=jnp.float32
    ).astype(jnp.bfloat16)
    grad_normed = lax.psum_scatter(grads, "expert", scatter_dimension=0, tiled=True).astype(
        jnp.float32
    )

    def apply_norm(inputs):
        return norm_scale(inputs, gain_row)

    primal, pullback = jax.vjp(apply_norm, saved_input[0].astype(jnp.float32))
    input_gradient = (cotangent.astype(jnp.float32) + pullback(grad_normed)[0]).astype(jnp.bfloat16)
    return (forward_output[None], input_gradient[None])


def solution(mesh):
    row = P("section", "expert", None)
    block = P("section", "expert", None, None)
    in_specs = (row, row, row, block, P("section", None), row, row, row, row, block, block)
    return jax.shard_map(
        local, mesh=mesh, in_specs=in_specs, out_specs=(row, row), check_vma=False
    )
```

time: 439 us -> 299 us (0.68); the launches traced: 432 us -> 298 us
  blocking collectives: 152 us -> 14.3 us
  local copies, waits for them, and re-layouts: 62.3 us -> 1.55 us
  waiting for transfers between devices: 143 us -> 201 us
  matrix products: 33.2 us -> 50 us
  other arithmetic: 23 us -> 8.72 us
  between operations: 1.31 us -> 14 us
  starting transfers between devices: 17.6 us -> 8.75 us
    all_to_all x2 -> x0, blocking collectives: 152 us -> none  [the longest x1 76.8 us: local(): lax.all_to_all(send_backward, 'expert', split_axis=0, concat_axis=0, tile...]
    all_to_all x2 -> x0, waiting for transfers between devices: 125 us -> none  [the longest x1 70 us: local(): lax.all_to_all(served_rows, 'expert', split_axis=0, concat_axis=0, tiled=...]
    reduce_scatter x0 -> x2, waiting for transfers between devices: none -> 90 us  [the longest x1 53.9 us: local(): lax.psum_scatter(served, 'expert', scatter_dimension=0, tiled=True)]
    all_gather x0 -> x2, waiting for transfers between devices: none -> 85.2 us  [the longest x1 50 us: local(): all_normed = lax.all_gather(normed, 'expert', axis=0, tiled=True)]
    reshape x10 -> x1, local copies, waits for them, and re-layouts: 28.1 us -> 0.09 us  [local(): routed = (weight_b > 0.0).reshape(peer_count, token_count)]
    dot_general x5, matrix products: 33.2 us -> 50 us  [the longest x1 18.4 us: local(): lax.dot_general(grad_both, weight_in, (((1,), (1,)), ((), ())), preferred...]
    all_gather x0 -> x1, blocking collectives: none -> 14.3 us  [local(): tables = lax.all_gather(table, 'expert', axis=0, tiled=True)]
    mul x6 -> x0, local copies, waits for them, and re-layouts: 10.3 us -> none  [the longest x2 9.87 us: local(): normalized(backward_gates[0])[:, :, None]]
  transfers between devices with their start and end apart: 4 -> 6, of which waited for: 4 -> 6; matrix products, arithmetic and copies ran while one was open for 2% -> 1% of each run, Pallas kernels for 0% -> 0%
where the time goes in v1:
time: 299 us; the launch traced here: 298 us
  waiting for transfers between devices  201 us (67%)
  matrix products  50 us (17%)
  blocking collectives  14.3 us (5%)
  between operations  14 us (5%)
  starting transfers between devices  8.75 us (3%)
  other arithmetic  8.72 us (3%)
    reduce_scatter x1, waiting for transfers between devices, local(): lax.psum_scatter(served, 'expert', scatter_dimension=0, tiled=True)  53.9 us
    all_gather x1, waiting for transfers between devices, local(): all_normed = lax.all_gather(normed, 'expert', axis=0, tiled=True)  50 us
    reduce_scatter x1, waiting for transfers between devices, local(): lax.psum_scatter(grads, 'expert', scatter_dimension=0, tiled=True)  36.1 us
    all_gather x1, waiting for transfers between devices, local(): all_cotangent = lax.all_gather(cotangent, 'expert', axis=0, tiled=True)  35.2 us
    ppermute x2, waiting for transfers between devices, passed_along(): lax.ppermute(value, axis, [(source, source + steps) for source in range(i...  25.8 us
    dot_general x1, matrix products, local(): lax.dot_general(grad_both, weight_in, (((1,), (1,)), ((), ())), preferred...  18.4 us
    all_gather x1, blocking collectives, local(): tables = lax.all_gather(table, 'expert', axis=0, tiled=True)  14.3 us
    dot_general x1, matrix products, local(): jnp.dot(all_normed, weight_in, preferred_element_type=jnp.float32)  11.5 us
  transfers between devices with their start and end apart: 6, of which 6 were waited for; matrix products, arithmetic and copies ran while one was open for 1% of the time, Pallas kernels for 0%

profile of v1, /device:TPU:0, one launch (start us, length us, event | category | flops | bytes accessed | tf_op | source)
XLA Modules:
  0.0 298.4 jit_solution(10791374151857974960)
XLA Ops:
  7.2 0.0 copy-start.5
  7.2 0.0 copy-start.6
  7.2 0.0 copy-start.7
  7.2 0.0 copy-start.8
  7.2 0.0 copy-start.2
  7.2 0.0 all-gather.7.cloned.1.call-start
  7.3 5.0 %collective-permute-start.1 = (bf16[1,72,4096]{2,1,0:T(8,128)(2,1)}, bf16[1,72,4096]{2,1,0:T(8,128)(2,1)S(1)}, u32[]{:S(2)}, u32[]{:S(2)}) collective-permute-start(bf16[1,72,4096]{2,1,0:T(8,128)(2,1)} %param.12), channel_id=1, source_target_pairs={{0,8},{8,16},{16,24},{1,9},{9,17},{17,25},{2,10},{10,18},{18,26},{... | collective-permute-start | bytes 1769480 | tf_op jit(solution)/shard_map/ppermute | solution.py:12
  12.3 12.8 %collective-permute-done.1 = bf16[1,72,4096]{2,1,0:T(8,128)(2,1)S(1)} collective-permute-done((bf16[1,72,4096]{2,1,0:T(8,128)(2,1)}, bf16[1,72,4096]{2,1,0:T(8,128)(2,1)S(1)}, u32[]{:S(2)}, u32[]{:S(2)}) %collective-permute-start.1) | collective-permute-done | bytes 589856 | tf_op jit(solution)/shard_map/ppermute | solution.py:12
  25.1 2.0 broadcast_select_fusion
  27.1 0.0 all-gather.7.cloned.1.call-update
  27.1 0.0 reduce-scatter.5.cloned.1.call-start
  27.2 0.0 copy-done.5
  27.2 0.0 copy-done.6
  27.2 0.0 copy-done.7
  27.3 0.0 copy-done.8
  27.3 14.3 %all-gather.1 = f32[8,72,16]{1,2,0:T(8,128)S(1)} all-gather(f32[1,72,16]{1,2,0:T(8,128)S(1)} %maximum_bitcast_fusion), channel_id=1, replica_groups=mesh['section'=4,'expert'=8] {'expert'}, dimensions={0}, use_global_device_ids=true | all-gather | bytes 41472 | tf_op jit(solution)/shard_map/all_gather | solution.py:49
  41.6 0.1 reshape.100
  41.7 0.0 copy-done.2
  41.7 0.3 reshape_squeeze.3
  42.1 0.1 reshape.92
  42.2 0.2 reduce_window_sum.11
  42.5 2.4 fusion.34
  44.9 35.2 %all-gather.7.cloned.1.call-done = bf16[1,576,4096]{2,1,0:T(8,128)(2,1)} async-done(((bf16[1,72,4096]{2,1,0:T(8,128)(2,1)}), bf16[1,576,4096]{2,1,0:T(8,128)(2,1)}) %all-gather.7.cloned.1.call-update) | async-done | bytes 4718608 | tf_op jit(solution)/shard_map/all_gather | solution.py:67
  80.1 9.4 %fusion.16 = (bf16[576,768]{1,0:T(8,128)(2,1)S(1)}, bf16[576,768]{1,0:T(8,128)(2,1)S(1)}) fusion(f32[576,1536]{1,0:T(8,128)} %bitcast.55, bf16[1,1,768,4096]{3,2,1,0:T(8,128)(2,1)} %param.21, bf16[1,576,4096]{2,1,0:T(8,128)(2,1)} %all-gather.7.cloned.1.call-done, f32[576]{0:T(1024)S(1)} %get-tuple-element.4), kind=kOutput, calls=%fused_computation.16 | convolution fusion | flops 3636707328 | bytes 16320768 | tf_op jit(solution)/shard_map/dot_general | solution.py:93
  89.6 18.4 %fusion.8 = bf16[576,4096]{1,0:T(8,128)(2,1)} fusion(bf16[1,1,4096,1536]{3,2,1,0:T(8,128)(2,1)} %param.20, bf16[576,768]{1,0:T(8,128)(2,1)S(1)} %get-tuple-element.9, bf16[576,768]{1,0:T(8,128)(2,1)S(1)} %get-tuple-element.8), kind=kOutput, calls=%fused_computation.10 | convolution fusion | flops 7253655552 | bytes 19070976 | tf_op jit(solution)/shard_map/dot_general | solution.py:101
  107.9 0.0 copy-start.3
  107.9 0.0 reduce-scatter.5.cloned.1.call-update
  107.9 0.0 copy-start.1
  107.9 0.0 copy-start.4
  108.0 0.0 copy-start
  108.0 0.0 all-gather.5.cloned.1.call-start
  108.0 1.0 copy-done.3
  109.0 3.4 %collective-permute-start = (bf16[1,72,4096]{2,1,0:T(8,128)(2,1)S(1)}, bf16[1,72,4096]{2,1,0:T(8,128)(2,1)S(1)}, u32[]{:S(2)}, u32[]{:S(2)}) collective-permute-start(bf16[1,72,4096]{2,1,0:T(8,128)(2,1)S(1)} %copy-done.3), channel_id=1, source_target_pairs={{0,8},{8,16},{16,24},{1,9},{9,17},{17,25},{2,10},{10,18},{18,26},{... | collective-permute-start | bytes 1769480 | tf_op jit(solution)/shard_map/ppermute | solution.py:12
  112.4 12.9 %collective-permute-done = bf16[1,72,4096]{2,1,0:T(8,128)(2,1)S(1)} collective-permute-done((bf16[1,72,4096]{2,1,0:T(8,128)(2,1)S(1)}, bf16[1,72,4096]{2,1,0:T(8,128)(2,1)S(1)}, u32[]{:S(2)}, u32[]{:S(2)}) %collective-permute-start) | collective-permute-done | bytes 589856 | tf_op jit(solution)/shard_map/ppermute | solution.py:12
  125.3 0.3 fusion.23
  125.6 36.1 %reduce-scatter.5.cloned.1.call-done = bf16[72,4096]{1,0:T(8,128)(2,1)} async-done(((bf16[576,4096]{1,0:T(8,128)(2,1)}), bf16[72,4096]{1,0:T(8,128)(2,1)}) %reduce-scatter.5.cloned.1.call-update) | async-done | bytes 589840 | tf_op jit(solution)/shard_map/reduce_scatter | solution.py:104
  161.7 0.0 copy-done.1
  161.7 0.0 copy-done.4
  161.7 1.4 fusion.27
  163.2 0.0 copy-done
  163.2 2.6 fusion.32
  165.9 0.0 all-gather.5.cloned.1.call-update
  165.9 0.2 reduce-scatter.3.cloned.1.call-start
  166.1 50.0 %all-gather.5.cloned.1.call-done = bf16[576,4096]{1,0:T(8,128)(2,1)} async-done(((bf16[72,4096]{1,0:T(8,128)(2,1)}), bf16[576,4096]{1,0:T(8,128)(2,1)}) %all-gather.5.cloned.1.call-update) | async-done | bytes 4718608 | tf_op jit(solution)/shard_map/all_gather | solution.py:66
  216.1 11.5 %fusion.2 = f32[576,1536]{1,0:T(8,128)S(1)} fusion(bf16[576,4096]{1,0:T(8,128)(2,1)} %all-gather.5.cloned.1.call-done, bf16[1,1,4096,1536]{3,2,1,0:T(8,128)(2,1)} %param.20), kind=kOutput, calls=%fused_computation.2 | convolution fusion | flops 7247757312 | bytes 20840448 | tf_op jit(solution)/shard_map/dot_general | solution.py:69
  227.5 8.4 %multiply_convert_fusion = bf16[576,4096]{1,0:T(8,128)(2,1)} fusion(bf16[1,1,768,4096]{3,2,1,0:T(8,128)(2,1)} %param.21, f32[576]{0:T(1024)S(1)} %get-tuple-element.5, f32[576,1536]{1,0:T(8,128)S(1)} %fusion.2), kind=kOutput, calls=%fused_computation.6 | convolution fusion | flops 3631251456 | bytes 14551296 | tf_op jit(solution)/shard_map/dot_general | solution.py:73
  235.9 0.0 reduce-scatter.3.cloned.1.call-update
  235.9 53.9 %reduce-scatter.3.cloned.1.call-done = bf16[72,4096]{1,0:T(8,128)(2,1)} async-done(((bf16[576,4096]{1,0:T(8,128)(2,1)}), bf16[72,4096]{1,0:T(8,128)(2,1)}) %reduce-scatter.3.cloned.1.call-update) | async-done | bytes 589840 | tf_op jit(solution)/shard_map/reduce_scatter | solution.py:75
  289.9 2.0 fusion.31
  (13 shorter events, 0.2 us)
Async XLA Ops:
  7.2 20.0 %copy-start.5 = (f32[1,72,4]{1,2,0:T(4,128)S(1)}, f32[1,72,4]{1,2,0:T(4,128)}, u32[]{:S(2)}) copy-start(f32[1,72,4]{1,2,0:T(4,128)} %param.19) | copy-start | bytes 3460
  7.2 20.0 %copy-start.6 = (f32[1,72,4]{1,2,0:T(4,128)S(1)}, f32[1,72,4]{1,2,0:T(4,128)}, u32[]{:S(2)}) copy-start(f32[1,72,4]{1,2,0:T(4,128)} %param.17) | copy-start | bytes 3460
  7.2 20.1 %copy-start.7 = (s32[1,72,4]{1,2,0:T(4,128)S(1)}, s32[1,72,4]{1,2,0:T(4,128)}, u32[]{:S(2)}) copy-start(s32[1,72,4]{1,2,0:T(4,128)} %param.18) | copy-start | bytes 3460
  7.2 20.1 %copy-start.8 = (s32[1,72,4]{1,2,0:T(4,128)S(1)}, s32[1,72,4]{1,2,0:T(4,128)}, u32[]{:S(2)}) copy-start(s32[1,72,4]{1,2,0:T(4,128)} %param.16) | copy-start | bytes 3460
  7.2 34.5 %copy-start.2 = (bf16[1,1,360,1536]{3,2,1,0:T(8,128)(2,1)S(1)}, bf16[1,1,360,1536]{3,2,1,0:T(8,128)(2,1)}, u32[]{:S(2)}) copy-start(bf16[1,1,360,1536]{3,2,1,0:T(8,128)(2,1)} %param.14) | copy-start | bytes 3317764
  7.2 72.9 %all-gather.7.cloned.1.call-start = ((), (), s32[]{:S(2)}) async-start(), calls=%async_computation.5 | async-start | bytes 5308416 | tf_op jit(solution)/shard_map/all_gather | solution.py:67
  7.3 17.9 %collective-permute-start.1 = (bf16[1,72,4096]{2,1,0:T(8,128)(2,1)}, bf16[1,72,4096]{2,1,0:T(8,128)(2,1)S(1)}, u32[]{:S(2)}, u32[]{:S(2)}) collective-permute-start(bf16[1,72,4096]{2,1,0:T(8,128)(2,1)} %param.12), channel_id=1, source_target_pairs={{0,8},{8,16},{16,24},{1,9},{9,17},{17,25},{2,10},{10,18},{18,26},{... | collective-permute-start | bytes 1769480 | tf_op jit(solution)/shard_map/ppermute | solution.py:12
  27.1 134.6 %reduce-scatter.5.cloned.1.call-start = ((), (), s32[]{:S(2)}) async-start(), calls=%async_computation.4 | async-start | bytes 5308416 | tf_op jit(solution)/shard_map/reduce_scatter | solution.py:104
  107.9 1.1 copy-start.3
  107.9 53.8 %copy-start.1 = (bf16[1,72,4096]{2,1,0:T(8,128)(2,1)S(1)}, bf16[1,72,4096]{2,1,0:T(8,128)(2,1)}, u32[]{:S(2)}) copy-start(bf16[1,72,4096]{2,1,0:T(8,128)(2,1)} %param.13) | copy-start | bytes 1769476
  107.9 53.8 %copy-start.4 = (f32[1,4096]{1,0:T(1,128)S(1)}, f32[1,4096]{1,0:T(1,128)}, u32[]{:S(2)}) copy-start(f32[1,4096]{1,0:T(1,128)} %param.15) | copy-start | bytes 49156
  108.0 55.2 %copy-start = (bf16[1,72,4096]{2,1,0:T(8,128)(2,1)S(1)}, bf16[1,72,4096]{2,1,0:T(8,128)(2,1)}, u32[]{:S(2)}) copy-start(bf16[1,72,4096]{2,1,0:T(8,128)(2,1)} %broadcast_select_fusion) | copy-start | bytes 1769476
  108.0 108.1 %all-gather.5.cloned.1.call-start = ((), (), s32[]{:S(2)}) async-start(), calls=%async_computation.2 | async-start | bytes 5308416 | tf_op jit(solution)/shard_map/all_gather | solution.py:66
  109.0 16.3 %collective-permute-start = (bf16[1,72,4096]{2,1,0:T(8,128)(2,1)S(1)}, bf16[1,72,4096]{2,1,0:T(8,128)(2,1)S(1)}, u32[]{:S(2)}, u32[]{:S(2)}) collective-permute-start(bf16[1,72,4096]{2,1,0:T(8,128)(2,1)S(1)} %copy-done.3), channel_id=1, source_target_pairs={{0,8},{8,16},{16,24},{1,9},{9,17},{17,25},{2,10},{10,18},{18,26},{... | collective-permute-start | bytes 1769480 | tf_op jit(solution)/shard_map/ppermute | solution.py:12
  165.9 124.0 %reduce-scatter.3.cloned.1.call-start = ((), (), s32[]{:S(2)}) async-start(), calls=%async_computation.3 | async-start | bytes 5308416 | tf_op jit(solution)/shard_map/reduce_scatter | solution.py:75
Sparse Core Ops, SparseCore 0:
  27.2 52.8 all-gather.6
  108.1 53.6 reduce-scatter.4
  166.0 50.0 all-gather.4
  236.1 53.7 reduce-scatter.2

commit v2 on v1

--- a/solution.py
+++ b/solution.py
@@ -1,6 +1,10 @@
+import functools
+
 import jax
 import jax.numpy as jnp
 from jax import lax
+from jax.experimental import pallas as pl
+from jax.experimental.pallas import tpu as pltpu
 from jax.sharding import PartitionSpec as P
 
 EPSILON = 1e-06
@@ -24,7 +28,7 @@
     return jnp.sum(jnp.where(onehot, weights[:, :, None], 0.0), axis=1)
 
 
-def local(
+def local_plain(
     forward_input,
     backward_cotangent,
     saved_input,
@@ -113,6 +117,513 @@
     return (forward_output[None], input_gradient[None])
 
 
+VMEM_LIMIT = 60 * 1024 * 1024
+CHUNKS = 4
+LANES = 128
+
+
+def relay_kernel(
+    sections, chips, tokens, width, hidden, capacity,
+    fin_ref, cot_ref, saved_ref, gain_ref, table_ref, stored_ref, win_hbm, wdown_hbm,
+    out_ref, grad_ref,
+    win, wdown, ct, xs, own_cot, layer, tables, wf, wb, proj, both, slots_b, slots_f, chain_b, chain_f, acc,
+    w_sem, t_send, t_recv, sh_send, sh_recv,
+    b_right, b_left, b_sib, b_recv, b_srecv,
+    f_right, f_left, f_sib, f_recv, f_srecv,
+    zb_send, zb_recv, zb_ss, zb_sr,
+    zf_send, zf_recv, zf_ss, zf_sr,
+):
+    peers = 2 * chips
+    section = lax.axis_index("section")
+    me = lax.axis_index("expert")
+    chip, core = me // 2, me % 2
+    sibling = chip * 2 + 1 - core
+    right = jnp.minimum(me + 2, peers - 1)
+    left = jnp.maximum(me - 2, 0)
+    cols = width // CHUNKS
+    base = core * chips
+    other = (1 - core) * chips
+    mine = base + chip
+    has_left, has_right = chip > 0, chip < chips - 1
+
+    def span(k):
+        return pl.ds(pl.multiple_of(k * cols, LANES), cols)
+
+    def expert_copy(src, dst, send, recv, peer):
+        return pltpu.make_async_remote_copy(
+            src_ref=src, dst_ref=dst, send_sem=send, recv_sem=recv,
+            device_id={"expert": peer}, device_id_type=pl.DeviceIdType.MESH,
+        )
+
+    barrier = pltpu.get_barrier_semaphore()
+    for step in range(1, peers):
+        pl.semaphore_signal(
+            barrier, inc=1, device_id={"expert": lax.rem(me + step, peers)},
+            device_id_type=pl.DeviceIdType.MESH,
+        )
+
+    @pl.when(section > 0)
+    def _():
+        pl.semaphore_signal(barrier, inc=1, device_id={"section": section - 1}, device_id_type=pl.DeviceIdType.MESH)
+
+    @pl.when(section < sections - 1)
+    def _():
+        pl.semaphore_signal(barrier, inc=1, device_id={"section": section + 1}, device_id_type=pl.DeviceIdType.MESH)
+
+    arrivals = jnp.where(section > 0, 1, 0) + jnp.where(section < sections - 1, 1, 0)
+    pl.semaphore_wait(barrier, arrivals + peers - 1)
+
+    following = jnp.minimum(section + 1, sections - 1)
+
+    def shift_cot(k):
+        return pltpu.make_async_remote_copy(
+            src_ref=cot_ref.at[:, span(k)], dst_ref=ct.at[mine, :, span(k)],
+            send_sem=sh_send.at[k], recv_sem=sh_recv.at[k],
+            device_id={"section": following}, device_id_type=pl.DeviceIdType.MESH,
+        )
+
+    shift_in = pltpu.make_async_remote_copy(
+        src_ref=fin_ref, dst_ref=layer, send_sem=sh_send.at[CHUNKS], recv_sem=sh_recv.at[CHUNKS],
+        device_id={"section": following}, device_id_type=pl.DeviceIdType.MESH,
+    )
+
+    @pl.when(section < sections - 1)
+    def _():
+        for k in range(CHUNKS):
+            shift_cot(k).start()
+        shift_in.start()
+
+    copy_down = pltpu.make_async_copy(wdown_hbm, wdown, w_sem.at[0])
+    copy_in = pltpu.make_async_copy(win_hbm, win, w_sem.at[1])
+    copy_down.start()
+    copy_in.start()
+
+    def table_copy(step):
+        peer = lax.rem(me + step, peers)
+        return expert_copy(table_ref, tables.at[mine], t_send.at[step], t_recv.at[step], peer)
+
+    for step in range(1, peers):
+        table_copy(step).start()
+
+    @pl.when(section == 0)
+    def _():
+        ct[mine] = cot_ref[...]
+        layer[...] = fin_ref[...]
+
+    tables[mine] = table_ref[...]
+
+    def gather_copies(buf, sems, block, k):
+        s_right, s_left, s_sib, recv, s_recv = sems
+        view = buf.at[base + block, :, span(k)]
+        return (
+            expert_copy(view, view, s_right.at[block, k], recv.at[block, k], right),
+            expert_copy(view, view, s_left.at[block, k], recv.at[block, k], left),
+            expert_copy(view, view, s_sib.at[block, k], s_recv.at[block, k], sibling),
+        )
+
+    def sibling_arrival(buf, sems, block, k):
+        s_sib, s_recv = sems[2], sems[4]
+        view = buf.at[other + block, :, span(k)]
+        return expert_copy(view, view, s_sib.at[block, k], s_recv.at[block, k], sibling)
+
+    def gather_own(buf, sems, k):
+        to_right, to_left, to_sib = gather_copies(buf, sems, chip, k)
+
+        @pl.when(has_right)
+        def _():
+            to_right.start()
+
+        @pl.when(has_left)
+        def _():
+            to_left.start()
+
+        to_sib.start()
+
+    def gather_relay(buf, sems, k):
+        for hop in range(1, chips):
+            @pl.when(chip >= hop)
+            def _():
+                to_right, _, to_sib = gather_copies(buf, sems, chip - hop, k)
+                to_right.wait_recv()
+
+                @pl.when(has_right)
+                def _():
+                    to_right.start()
+
+                to_sib.start()
+
+            @pl.when(chip + hop < chips)
+            def _():
+                _, to_left, to_sib = gather_copies(buf, sems, chip + hop, k)
+                to_left.wait_recv()
+
+                @pl.when(has_left)
+                def _():
+                    to_left.start()
+
+                to_sib.start()
+
+        for block in range(chips):
+            sibling_arrival(buf, sems, block, k).wait_recv()
+
+    def gather_drain(buf, sems, k):
+        for block in range(chips):
+            to_right, to_left, to_sib = gather_copies(buf, sems, block, k)
+
+            @pl.when(has_right & (block <= chip))
+            def _():
+                to_right.wait_send()
+
+            @pl.when(has_left & (block >= chip))
+            def _():
+                to_left.wait_send()
+
+            to_sib.wait_send()
+
+    def cross_copy(buf, slots, sems, k):
+        return expert_copy(
+            buf.at[pl.ds(other, chips), :, span(k)], slots.at[:, :, span(k)],
+            sems[2].at[k], sems[3].at[k], sibling,
+        )
+
+    def chain_copy(buf, chain, sems, dest, slot, k, peer):
+        return expert_copy(
+            buf.at[base + dest, :, span(k)], chain.at[slot, :, span(k)],
+            sems[0].at[dest, k], sems[1].at[slot, k], peer,
+        )
+
+    def chain_step(buf, slots, chain, sems, hop, k):
+        def advance(dest, slot, source_exists, peer):
+            value = buf[base + dest, :, span(k)].astype(jnp.float32) + slots[
+                dest, :, span(k)
+            ].astype(jnp.float32)
+            buf[base + dest, :, span(k)] = value.astype(jnp.bfloat16)
+
+            @pl.when(source_exists)
+            def _():
+                chain_copy(buf, chain, sems, dest, slot, k, peer).wait_recv()
+                buf[base + dest, :, span(k)] = (
+                    value + chain[slot, :, span(k)].astype(jnp.float32)
+                ).astype(jnp.bfloat16)
+
+            chain_copy(buf, chain, sems, dest, slot, k, peer).start()
+
+        @pl.when(chip <= hop)
+        def _():
+            dest = chips - 1 - hop + chip
+            advance(dest, dest + 1, has_left, right)
+
+        @pl.when(chips - 1 - chip <= hop)
+        def _():
+            dest = hop - (chips - 1 - chip)
+            advance(dest, dest, has_right, left)
+
+    def chain_end(buf, slots, chain, sems, k):
+        total = acc.at[0 if buf is ct else 1]
+        total[:, span(k)] = buf[mine, :, span(k)].astype(jnp.float32) + slots[
+            chip, :, span(k)
+        ].astype(jnp.float32)
+
+        @pl.when(has_left)
+        def _():
+            chain_copy(buf, chain, sems, chip, chip + 1, k, right).wait_recv()
+            total[:, span(k)] += chain[chip + 1, :, span(k)].astype(jnp.float32)
+
+        @pl.when(has_right)
+        def _():
+            chain_copy(buf, chain, sems, chip, chip, k, left).wait_recv()
+            total[:, span(k)] += chain[chip, :, span(k)].astype(jnp.float32)
+
+    def chain_round(buf, slots, chain, sems, step):
+        for hop in range(chips):
+            k = step - hop
+
+            @pl.when((k >= 0) & (k < CHUNKS))
+            def _():
+                if hop == 0:
+                    cross_copy(buf, slots, sems, k).wait_recv()
+                if hop < chips - 1:
+                    chain_step(buf, slots, chain, sems, hop, k)
+                else:
+                    chain_end(buf, slots, chain, sems, k)
+
+    def chain_drain(buf, slots, chain, sems, k):
+        cross_copy(buf, slots, sems, k).wait_send()
+        for dest in range(chips):
+            @pl.when(chip != dest)
+            def _():
+                chain_copy(buf, chain, sems, dest, dest, k, left).wait_send()
+
+    def loop(count, body):
+        def wrapped(k, carry):
+            body(k)
+            return carry
+
+        lax.fori_loop(0, count, wrapped, 0)
+
+    back = (b_right, b_left, b_sib, b_recv, b_srecv)
+    ahead = (f_right, f_left, f_sib, f_recv, f_srecv)
+    back_sum = (zb_send, zb_recv, zb_ss, zb_sr)
+    ahead_sum = (zf_send, zf_recv, zf_ss, zf_sr)
+
+    def first(k):
+        @pl.when(section > 0)
+        def _():
+            shift_cot(k).wait_recv()
+
+        gather_own(ct, back, k)
+
+    loop(CHUNKS, first)
+
+    @pl.when(section > 0)
+    def _():
+        shift_in.wait_recv()
+
+    widened = layer[...].astype(jnp.float32)
+    inverse = lax.rsqrt(jnp.mean(widened * widened, axis=-1, keepdims=True) + EPSILON)
+    xs[mine] = (widened * inverse * gain_ref[...]).astype(jnp.bfloat16)
+    own_cot[...] = ct[mine]
+
+    for step in range(1, peers):
+        table_copy(step).wait_recv()
+    lane = lax.broadcasted_iota(jnp.int32, (tokens, LANES), 1)
+    for block in range(peers):
+        values = tables[block]
+        rows = pl.ds(block * tokens, tokens)
+        wf[rows, :] = jnp.sum(jnp.where(lane == me, values, 0.0), axis=1, keepdims=True)
+        wb[rows, :] = jnp.sum(jnp.where(lane == me + peers, values, 0.0), axis=1, keepdims=True)
+
+    copy_down.wait()
+
+    def widen(buf, k):
+        return jnp.concatenate(
+            [buf[block, :, span(k)].astype(jnp.float32) for block in range(peers)], axis=0
+        )
+
+    def spread(buf, k, value):
+        for block in range(peers):
+            buf[block, :, span(k)] = value[block * tokens : (block + 1) * tokens].astype(
+                jnp.bfloat16
+            )
+
+    def gather_back(k):
+        gather_relay(ct, back, k)
+        scaled = (widen(ct, k) * wb[...]).astype(jnp.bfloat16)
+        part = lax.dot_general(
+            scaled, wdown[:, span(k)], (((1,), (1,)), ((), ())), preferred_element_type=jnp.float32
+        )
+
+        @pl.when(k == 0)
+        def _():
+            proj[:, :hidden] = part
+
+        @pl.when(k > 0)
+        def _():
+            proj[:, :hidden] += part
+
+    loop(CHUNKS, gather_back)
+    gather_own(xs, ahead, 0)
+    loop(CHUNKS, functools.partial(gather_drain, ct, back))
+
+    lower = (
+        lax.broadcasted_iota(jnp.int32, (tokens, tokens), 1)
+        < lax.broadcasted_iota(jnp.int32, (tokens, tokens), 0)
+    ).astype(jnp.bfloat16)
+    slot_total = stored_ref.shape[0]
+    place = lax.broadcasted_iota(jnp.int32, (tokens, slot_total), 1).astype(jnp.float32)
+
+    def hidden_grads(block):
+        rows = pl.ds(pl.multiple_of(block * tokens, 8), tokens)
+        routed = wb[rows, :] > 0.0
+        marks = jnp.where(routed, 1.0, 0.0)
+        wide_marks = jnp.broadcast_to(marks, (tokens, LANES)).astype(jnp.bfloat16)
+        rank = jnp.dot(lower, wide_marks, preferred_element_type=jnp.float32)[:, :1]
+        source = (block % chips) * 2 + block // chips
+        slot = rank + (source * capacity).astype(jnp.float32)
+        pick = jnp.where((place == slot) & (marks > 0.0), 1.0, 0.0).astype(jnp.bfloat16)
+        stored = jnp.dot(pick, stored_ref[...], preferred_element_type=jnp.float32)
+        gate, up = stored[:, :hidden], stored[:, hidden:]
+        grad_hidden = proj[rows, :hidden]
+        sig = jax.nn.sigmoid(gate)
+        both[block, :, :hidden] = (
+            grad_hidden * up * sig * (1.0 + gate * (1.0 - sig))
+        ).astype(jnp.bfloat16)
+        both[block, :, hidden:] = (grad_hidden * gate * sig).astype(jnp.bfloat16)
+
+    loop(peers, hidden_grads)
+    copy_in.wait()
+
+    def all_rows():
+        return jnp.concatenate(
+            [both[block].astype(jnp.float32) for block in range(peers)], axis=0
+        ).astype(jnp.bfloat16)
+
+    def middle(k):
+        @pl.when(k + 1 < CHUNKS)
+        def _():
+            gather_own(xs, ahead, k + 1)
+
+        rows = pl.ds(pl.multiple_of(k * cols, LANES), cols)
+        spread(
+            ct, k,
+            lax.dot_general(
+                all_rows(), win[rows, :], (((1,), (1,)), ((), ())),
+                preferred_element_type=jnp.float32,
+            ),
+        )
+        cross_copy(ct, slots_b, back_sum, k).start()
+        gather_relay(xs, ahead, k)
+        chain_round(ct, slots_b, chain_b, back_sum, k)
+        part = jnp.dot(
+            widen(xs, k).astype(jnp.bfloat16), win[rows, :], preferred_element_type=jnp.float32
+        )
+
+        @pl.when(k == 0)
+        def _():
+            proj[...] = part
+
+        @pl.when(k > 0)
+        def _():
+            proj[...] += part
+
+    loop(CHUNKS, middle)
+    loop(CHUNKS, functools.partial(gather_drain, xs, ahead))
+
+    def activate(block):
+        rows = pl.ds(pl.multiple_of(block * tokens, 8), tokens)
+        gate, up = proj[rows, :hidden], proj[rows, hidden:]
+        both[block, :, :hidden] = (gate / (1.0 + jnp.exp(-gate)) * up).astype(jnp.bfloat16)
+
+    loop(peers, activate)
+
+    def serve(k):
+        active = jnp.concatenate(
+            [both[block, :, :hidden].astype(jnp.float32) for block in range(peers)], axis=0
+        ).astype(jnp.bfloat16)
+        value = jnp.dot(active, wdown[:, span(k)], preferred_element_type=jnp.float32)
+        spread(xs, k, value * wf[...])
+        cross_copy(xs, slots_f, ahead_sum, k).start()
+        chain_round(xs, slots_f, chain_f, ahead_sum, k)
+
+        @pl.when(k + CHUNKS < CHUNKS + chips - 1)
+        def _():
+            chain_round(ct, slots_b, chain_b, back_sum, k + CHUNKS)
+
+    loop(CHUNKS, serve)
+    for step in range(2 * CHUNKS, CHUNKS + chips - 1):
+        chain_round(ct, slots_b, chain_b, back_sum, step)
+
+    saved = saved_ref[...].astype(jnp.float32)
+    inverse = lax.rsqrt(jnp.mean(saved * saved, axis=-1, keepdims=True) + EPSILON)
+    pulled = acc[0] * gain_ref[...]
+    along = jnp.mean(saved * pulled, axis=-1, keepdims=True)
+    grad_ref[...] = (
+        own_cot[...].astype(jnp.float32) + inverse * (pulled - saved * (inverse * inverse * along))
+    ).astype(jnp.bfloat16)
+
+    def last(step):
+        chain_round(xs, slots_f, chain_f, ahead_sum, step + CHUNKS)
+
+    loop(chips - 1, last)
+    out_ref[...] = (layer[...].astype(jnp.float32) + acc[1]).astype(jnp.bfloat16)
+
+    loop(CHUNKS, functools.partial(chain_drain, ct, slots_b, chain_b, back_sum))
+    loop(CHUNKS, functools.partial(chain_drain, xs, slots_f, chain_f, ahead_sum))
+    for step in range(1, peers):
+        table_copy(step).wait_send()
+
+    @pl.when(section < sections - 1)
+    def _():
+        for k in range(CHUNKS):
+            shift_cot(k).wait_send()
+        shift_in.wait_send()
+
+
+def local_fused(
+    forward_input,
+    backward_cotangent,
+    saved_input,
+    saved_hidden,
+    norm_gain,
+    forward_experts,
+    forward_gates,
+    backward_experts,
+    backward_gates,
+    gate_up_weight,
+    down_weight,
+):
+    peers = lax.axis_size("expert")
+    chips = peers // 2
+    tokens, width = forward_input.shape[1:]
+    hidden = down_weight.shape[2]
+    slot_total = saved_hidden.shape[2]
+    table = jnp.concatenate(
+        [
+            dense_weights(forward_experts[0], forward_gates[0], peers),
+            dense_weights(backward_experts[0], backward_gates[0], peers),
+            jnp.zeros((tokens, LANES - 2 * peers), jnp.float32),
+        ],
+        axis=1,
+    )
+    rows = peers * tokens
+    bf16, f32 = jnp.bfloat16, jnp.float32
+    dma = pltpu.SemaphoreType.DMA
+    gather_sems = [dma((chips, CHUNKS))] * 5
+    sum_sems = [dma((chips, CHUNKS)), dma((chips + 1, CHUNKS)), dma((CHUNKS,)), dma((CHUNKS,))]
+    vmem = pl.BlockSpec(memory_space=pltpu.VMEM)
+    hbm = pl.BlockSpec(memory_space=pl.ANY)
+    out = jax.ShapeDtypeStruct((tokens, width), bf16)
+    forward_output, input_gradient = pl.pallas_call(
+        functools.partial(
+            relay_kernel, lax.axis_size("section"), chips, tokens, width, hidden, slot_total // peers
+        ),
+        out_shape=(out, out),
+        in_specs=[vmem] * 6 + [hbm] * 2,
+        out_specs=(vmem, vmem),
+        scratch_shapes=[
+            pltpu.VMEM((width, 2 * hidden), bf16),
+            pltpu.VMEM((hidden, width), bf16),
+            pltpu.VMEM((peers, tokens, width), bf16),
+            pltpu.VMEM((peers, tokens, width), bf16),
+            pltpu.VMEM((tokens, width), bf16),
+            pltpu.VMEM((tokens, width), bf16),
+            pltpu.VMEM((peers, tokens, LANES), f32),
+            pltpu.VMEM((rows, 1), f32),
+            pltpu.VMEM((rows, 1), f32),
+            pltpu.VMEM((rows, 2 * hidden), f32),
+            pltpu.VMEM((peers, tokens, 2 * hidden), bf16),
+            pltpu.VMEM((chips, tokens, width), bf16),
+            pltpu.VMEM((chips, tokens, width), bf16),
+            pltpu.VMEM((chips + 1, tokens, width), bf16),
+            pltpu.VMEM((chips + 1, tokens, width), bf16),
+            pltpu.VMEM((2, tokens, width), f32),
+            dma((2,)),
+            dma((peers,)),
+            dma((peers,)),
+            dma((CHUNKS + 1,)),
+            dma((CHUNKS + 1,)),
+        ]
+        + gather_sems + gather_sems + sum_sems + sum_sems,
+        compiler_params=pltpu.CompilerParams(
+            collective_id=0, has_side_effects=True, vmem_limit_bytes=VMEM_LIMIT
+        ),
+    )(
+        forward_input[0], backward_cotangent[0], saved_input[0], norm_gain, table,
+        saved_hidden[0, 0], gate_up_weight[0, 0], down_weight[0, 0],
+    )
+    return (forward_output[None], input_gradient[None])
+
+
+def local(*arrays):
+    peers = lax.axis_size("expert")
+    tokens, width = arrays[0].shape[1:]
+    hidden = arrays[10].shape[2]
+    weights = 6 * hidden * width
+    buffers = (2 * peers + 2 * (peers + 1)) * tokens * width * 2
+    fits = weights + buffers < VMEM_LIMIT * 3 // 4
+    return (local_fused if fits and peers % 2 == 0 else local_plain)(*arrays)
+
+
 def solution(mesh):
     row = P("section", "expert", None)
     block = P("section", "expert", None, None)

time: 299 us -> 193 us (0.65)
  the two profiles are of different devices: /device:TPU:0 before, /device:TPU:13 now
where the time goes in v2:
time: 193 us; the launch traced here: 192 us
  Pallas kernels  183 us (95%)
  other arithmetic  4.86 us (3%)
  local copies, waits for them, and re-layouts  4.09 us (2%)
    pallas_call x1, Pallas kernels, local_fused(): pl.pallas_call(functools.partial(relay_kernel, lax.axis_size('section'),...  183 us

profile of v2, /device:TPU:13, one launch (start us, length us, event | category | flops | bytes accessed | tf_op | source)
XLA Modules:
  0.0 192.1 jit_solution(11960588174787902638)
XLA Ops:
  0.6 0.7 reduce_sum.36
  1.3 0.7 reduce_sum.38
  2.0 0.1 pad.2.clone
  2.1 0.7 bitcast_divide_fusion
  2.8 0.7 bitcast_divide_fusion.1
  3.5 0.7 select_reduce_fusion.1
  4.2 0.7 select_reduce_fusion
  4.9 0.1 copy.18
  5.0 0.1 copy.17
  5.0 0.7 maximum_maximum_fusion.table_ref
  5.7 182.5 %shard_map.122 = (bf16[72,4096]{1,0:T(8,128)(2,1)}, bf16[72,4096]{1,0:T(8,128)(2,1)}) custom-call(bf16[72,4096]{1,0:T(8,128)(2,1)} %bitcast.17, bf16[72,4096]{1,0:T(8,128)(2,1)} %bitcast.18, bf16[72,4096]{1,0:T(8,128)(2,1)} %bitcast.19, f32[1,4096]{1,0:T(1,128)} %gain_ref.1, f32[72,128]{1,0:T(8,128)} %maximum_maximum_fusion.table_ref, ...), custom_call_target="tpu_custom_call" | custom-call | tf_op jit(solution)/shard_map/pallas_call | solution.py:576
  188.3 1.9 copy.21
  190.2 1.9 copy.22
  (1 shorter events, 0.0 us)

commit v3 on v2

--- a/solution.py
+++ b/solution.py
@@ -124,12 +124,11 @@
 
 def relay_kernel(
     sections, chips, tokens, width, hidden, capacity,
-    fin_ref, cot_ref, saved_ref, gain_ref, table_ref, stored_ref, win_hbm, wdown_hbm,
+    fin_ref, cot_ref, saved_ref, gain_ref, fid_ref, fgate_ref, bid_ref, bgate_ref, stored_ref, win_hbm, wdown_hbm,
     out_ref, grad_ref,
-    win, wdown, ct, xs, own_cot, layer, tables, wf, wb, proj, both, slots_b, slots_f, chain_b, chain_f, acc,
+    win, wdown, pool, own_cot, layer, table_ref, tables, wf, wb, proj, both, slots_b, slots_f, chain_b, chain_f, acc,
     w_sem, t_send, t_recv, sh_send, sh_recv,
-    b_right, b_left, b_sib, b_recv, b_srecv,
-    f_right, f_left, f_sib, f_recv, f_srecv,
+    s_right, s_left, s_sib, g_recv, g_srecv,
     zb_send, zb_recv, zb_ss, zb_sr,
     zf_send, zf_recv, zf_ss, zf_sr,
 ):
@@ -145,6 +144,7 @@
     other = (1 - core) * chips
     mine = base + chip
     has_left, has_right = chip > 0, chip < chips - 1
+    ct, xs = pool.at[pl.ds(0, peers)], pool.at[pl.ds(peers, peers)]
 
     def span(k):
         return pl.ds(pl.multiple_of(k * cols, LANES), cols)
@@ -191,13 +191,26 @@
     def _():
         for k in range(CHUNKS):
             shift_cot(k).start()
-        shift_in.start()
 
     copy_down = pltpu.make_async_copy(wdown_hbm, wdown, w_sem.at[0])
     copy_in = pltpu.make_async_copy(win_hbm, win, w_sem.at[1])
     copy_down.start()
     copy_in.start()
 
+    lane = lax.broadcasted_iota(jnp.int32, (tokens, LANES), 1)
+
+    def dense(ids, gates, offset):
+        weights = gates / jnp.sum(gates, axis=-1, keepdims=True)
+        total = jnp.zeros((tokens, LANES), jnp.float32)
+        for choice in range(ids.shape[1]):
+            hit = lane == ids[:, choice : choice + 1] + offset
+            total += jnp.where(hit, weights[:, choice : choice + 1], 0.0)
+        return total
+
+    table_ref[...] = dense(fid_ref[...], fgate_ref[...], 0) + dense(
+        bid_ref[...], bgate_ref[...], peers
+    )
+
     def table_copy(step):
         peer = lax.rem(me + step, peers)
         return expert_copy(table_ref, tables.at[mine], t_send.at[step], t_recv.at[step], peer)
@@ -212,22 +225,20 @@
 
     tables[mine] = table_ref[...]
 
-    def gather_copies(buf, sems, block, k):
-        s_right, s_left, s_sib, recv, s_recv = sems
-        view = buf.at[base + block, :, span(k)]
+    def gather_copies(index, block):
+        which, k = index // CHUNKS, index % CHUNKS
+        view = pool.at[which * peers + base + block, :, span(k)]
+        recv = g_recv.at[which, block, k]
         return (
-            expert_copy(view, view, s_right.at[block, k], recv.at[block, k], right),
-            expert_copy(view, view, s_left.at[block, k], recv.at[block, k], left),
-            expert_copy(view, view, s_sib.at[block, k], s_recv.at[block, k], sibling),
-        )
-
-    def sibling_arrival(buf, sems, block, k):
-        s_sib, s_recv = sems[2], sems[4]
-        view = buf.at[other + block, :, span(k)]
-        return expert_copy(view, view, s_sib.at[block, k], s_recv.at[block, k], sibling)
-
-    def gather_own(buf, sems, k):
-        to_right, to_left, to_sib = gather_copies(buf, sems, chip, k)
+            expert_copy(view, view, s_right.at[which, block, k], recv, right),
+            expert_copy(view, view, s_left.at[which, block, k], recv, left),
+            expert_copy(
+                view, view, s_sib.at[which, block, k], g_srecv.at[which, block, k], sibling
+            ),
+        )
+
+    def gather_own(index):
+        to_right, to_left, to_sib = gather_copies(index, chip)
 
         @pl.when(has_right)
         def _():
@@ -239,36 +250,48 @@
 
         to_sib.start()
 
-    def gather_relay(buf, sems, k):
-        for hop in range(1, chips):
-            @pl.when(chip >= hop)
-            def _():
-                to_right, _, to_sib = gather_copies(buf, sems, chip - hop, k)
-                to_right.wait_recv()
-
-                @pl.when(has_right)
-                def _():
-                    to_right.start()
-
-                to_sib.start()
-
-            @pl.when(chip + hop < chips)
-            def _():
-                _, to_left, to_sib = gather_copies(buf, sems, chip + hop, k)
-                to_left.wait_recv()
-
-                @pl.when(has_left)
-                def _():
-                    to_left.start()
-
-                to_sib.start()
-
+    def gather_hop(index, hop):
+        @pl.when(chip >= hop)
+        def _():
+            to_right, _, to_sib = gather_copies(index, chip - hop)
+            to_right.wait_recv()
+
+            @pl.when(has_right)
+            def _():
+                to_right.start()
+
+            to_sib.start()
+
+        @pl.when(chip + hop < chips)
+        def _():
+            _, to_left, to_sib = gather_copies(index, chip + hop)
+            to_left.wait_recv()
+
+            @pl.when(has_left)
+            def _():
+                to_left.start()
+
+            to_sib.start()
+
+    def gather_round(step):
+        for hop in range(chips - 1, 0, -1):
+            index = step - hop + 1
+
+            @pl.when((index >= 0) & (index < 2 * CHUNKS))
+            def _():
+                gather_hop(index, hop)
+
+    def gather_end(index):
+        which, k = index // CHUNKS, index % CHUNKS
         for block in range(chips):
-            sibling_arrival(buf, sems, block, k).wait_recv()
-
-    def gather_drain(buf, sems, k):
+            view = pool.at[which * peers + other + block, :, span(k)]
+            expert_copy(
+                view, view, s_sib.at[which, block, k], g_srecv.at[which, block, k], sibling
+            ).wait_recv()
+
+    def gather_drain(index):
         for block in range(chips):
-            to_right, to_left, to_sib = gather_copies(buf, sems, block, k)
+            to_right, to_left, to_sib = gather_copies(index, block)
 
             @pl.when(has_right & (block <= chip))
             def _():
@@ -319,7 +342,7 @@
             advance(dest, dest, has_right, left)
 
     def chain_end(buf, slots, chain, sems, k):
-        total = acc.at[0 if buf is ct else 1]
+        total = acc.at[0 if sems is back_sum else 1]
         total[:, span(k)] = buf[mine, :, span(k)].astype(jnp.float32) + slots[
             chip, :, span(k)
         ].astype(jnp.float32)
@@ -335,7 +358,7 @@
             total[:, span(k)] += chain[chip, :, span(k)].astype(jnp.float32)
 
     def chain_round(buf, slots, chain, sems, step):
-        for hop in range(chips):
+        for hop in range(chips - 1, -1, -1):
             k = step - hop
 
             @pl.when((k >= 0) & (k < CHUNKS))
@@ -361,8 +384,6 @@
 
         lax.fori_loop(0, count, wrapped, 0)
 
-    back = (b_right, b_left, b_sib, b_recv, b_srecv)
-    ahead = (f_right, f_left, f_sib, f_recv, f_srecv)
     back_sum = (zb_send, zb_recv, zb_ss, zb_sr)
     ahead_sum = (zf_send, zf_recv, zf_ss, zf_sr)
 
@@ -371,28 +392,39 @@
         def _():
             shift_cot(k).wait_recv()
 
-        gather_own(ct, back, k)
-
-    loop(CHUNKS, first)
-
-    @pl.when(section > 0)
-    def _():
-        shift_in.wait_recv()
-
-    widened = layer[...].astype(jnp.float32)
-    inverse = lax.rsqrt(jnp.mean(widened * widened, axis=-1, keepdims=True) + EPSILON)
-    xs[mine] = (widened * inverse * gain_ref[...]).astype(jnp.bfloat16)
-    own_cot[...] = ct[mine]
+        gather_own(k)
+
+    lead = 2
+    span_rounds = chips - 2
+    loop(lead, first)
 
     for step in range(1, peers):
         table_copy(step).wait_recv()
-    lane = lax.broadcasted_iota(jnp.int32, (tokens, LANES), 1)
     for block in range(peers):
         values = tables[block]
         rows = pl.ds(block * tokens, tokens)
         wf[rows, :] = jnp.sum(jnp.where(lane == me, values, 0.0), axis=1, keepdims=True)
         wb[rows, :] = jnp.sum(jnp.where(lane == me + peers, values, 0.0), axis=1, keepdims=True)
 
+    @pl.when(section < sections - 1)
+    def _():
+        shift_in.start()
+
+    def opening(step):
+        first(step + lead)
+        gather_round(step)
+
+    loop(CHUNKS - lead, opening)
+
+    @pl.when(section > 0)
+    def _():
+        shift_in.wait_recv()
+
+    widened = layer[...].astype(jnp.float32)
+    inverse = lax.rsqrt(jnp.mean(widened * widened, axis=-1, keepdims=True) + EPSILON)
+    xs[mine] = (widened * inverse * gain_ref[...]).astype(jnp.bfloat16)
+    own_cot[...] = ct[mine]
+
     copy_down.wait()
 
     def widen(buf, k):
@@ -407,7 +439,19 @@
             )
 
     def gather_back(k):
-        gather_relay(ct, back, k)
+        @pl.when(k < CHUNKS)
+        def _():
+            gather_own(k + CHUNKS)
+
+        gather_round(k + CHUNKS - lead)
+        ready = k + CHUNKS - lead - span_rounds
+
+        @pl.when((ready >= 0) & (ready < CHUNKS))
+        def _():
+            gather_end(ready)
+            hidden_part(ready)
+
+    def hidden_part(k):
         scaled = (widen(ct, k) * wb[...]).astype(jnp.bfloat16)
         part = lax.dot_general(
             scaled, wdown[:, span(k)], (((1,), (1,)), ((), ())), preferred_element_type=jnp.float32
@@ -421,9 +465,9 @@
         def _():
             proj[:, :hidden] += part
 
-    loop(CHUNKS, gather_back)
-    gather_own(xs, ahead, 0)
-    loop(CHUNKS, functools.partial(gather_drain, ct, back))
+    opened = max(CHUNKS, lead + span_rounds)
+    loop(opened, gather_back)
+    loop(CHUNKS, gather_drain)
 
     lower = (
         lax.broadcasted_iota(jnp.int32, (tokens, tokens), 1)
@@ -459,10 +503,6 @@
         ).astype(jnp.bfloat16)
 
     def middle(k):
-        @pl.when(k + 1 < CHUNKS)
-        def _():
-            gather_own(xs, ahead, k + 1)
-
         rows = pl.ds(pl.multiple_of(k * cols, LANES), cols)
         spread(
             ct, k,
@@ -472,8 +512,9 @@
             ),
         )
         cross_copy(ct, slots_b, back_sum, k).start()
-        gather_relay(xs, ahead, k)
+        gather_round(k + opened + CHUNKS - lead)
         chain_round(ct, slots_b, chain_b, back_sum, k)
+        gather_end(k + CHUNKS)
         part = jnp.dot(
             widen(xs, k).astype(jnp.bfloat16), win[rows, :], preferred_element_type=jnp.float32
         )
@@ -487,7 +528,7 @@
             proj[...] += part
 
     loop(CHUNKS, middle)
-    loop(CHUNKS, functools.partial(gather_drain, xs, ahead))
+    loop(CHUNKS, lambda k: gather_drain(k + CHUNKS))
 
     def activate(block):
         rows = pl.ds(pl.multiple_of(block * tokens, 8), tokens)
@@ -557,18 +598,10 @@
     tokens, width = forward_input.shape[1:]
     hidden = down_weight.shape[2]
     slot_total = saved_hidden.shape[2]
-    table = jnp.concatenate(
-        [
-            dense_weights(forward_experts[0], forward_gates[0], peers),
-            dense_weights(backward_experts[0], backward_gates[0], peers),
-            jnp.zeros((tokens, LANES - 2 * peers), jnp.float32),
-        ],
-        axis=1,
-    )
     rows = peers * tokens
     bf16, f32 = jnp.bfloat16, jnp.float32
     dma = pltpu.SemaphoreType.DMA
-    gather_sems = [dma((chips, CHUNKS))] * 5
+    gather_sems = [dma((2, chips, CHUNKS))] * 5
     sum_sems = [dma((chips, CHUNKS)), dma((chips + 1, CHUNKS)), dma((CHUNKS,)), dma((CHUNKS,))]
     vmem = pl.BlockSpec(memory_space=pltpu.VMEM)
     hbm = pl.BlockSpec(memory_space=pl.ANY)
@@ -578,15 +611,15 @@
             relay_kernel, lax.axis_size("section"), chips, tokens, width, hidden, slot_total // peers
         ),
         out_shape=(out, out),
-        in_specs=[vmem] * 6 + [hbm] * 2,
+        in_specs=[vmem] * 9 + [hbm] * 2,
         out_specs=(vmem, vmem),
         scratch_shapes=[
             pltpu.VMEM((width, 2 * hidden), bf16),
             pltpu.VMEM((hidden, width), bf16),
-            pltpu.VMEM((peers, tokens, width), bf16),
-            pltpu.VMEM((peers, tokens, width), bf16),
+            pltpu.VMEM((2 * peers, tokens, width), bf16),
             pltpu.VMEM((tokens, width), bf16),
             pltpu.VMEM((tokens, width), bf16),
+            pltpu.VMEM((tokens, LANES), f32),
             pltpu.VMEM((peers, tokens, LANES), f32),
             pltpu.VMEM((rows, 1), f32),
             pltpu.VMEM((rows, 1), f32),
@@ -603,12 +636,13 @@
             dma((CHUNKS + 1,)),
             dma((CHUNKS + 1,)),
         ]
-        + gather_sems + gather_sems + sum_sems + sum_sems,
+        + gather_sems + sum_sems + sum_sems,
         compiler_params=pltpu.CompilerParams(
             collective_id=0, has_side_effects=True, vmem_limit_bytes=VMEM_LIMIT
         ),
     )(
-        forward_input[0], backward_cotangent[0], saved_input[0], norm_gain, table,
+        forward_input[0], backward_cotangent[0], saved_input[0], norm_gain,
+        forward_experts[0], forward_gates[0], backward_experts[0], backward_gates[0],
         saved_hidden[0, 0], gate_up_weight[0, 0], down_weight[0, 0],
     )
     return (forward_output[None], input_gradient[None])

time: 193 us -> 170 us (0.88)
  the two profiles are of different devices: /device:TPU:13 before, /device:TPU:0 now
where the time goes in v3:
time: 170 us
  Pallas kernels  160 us (94%)
  local copies, waits for them, and re-layouts  9.37 us (6%)
    pallas_call x1, Pallas kernels, local_fused(): pl.pallas_call(functools.partial(relay_kernel, lax.axis_size('section'),...  160 us
    unnamed x6, local copies, waits for them, and re-layouts  9.37 us

profile of v3, /device:TPU:0, one launch (start us, length us, event | category | flops | bytes accessed | tf_op | source)
XLA Modules:
  0.0 170.2 jit_solution(6217199509633429162)
XLA Ops:
  0.6 1.4 copy.13
  2.0 1.4 copy.14
  3.4 1.4 copy.15
  4.8 1.4 copy.16
  6.2 160.1 %shard_map.122 = (bf16[72,4096]{1,0:T(8,128)(2,1)}, bf16[72,4096]{1,0:T(8,128)(2,1)}) custom-call(bf16[72,4096]{1,0:T(8,128)(2,1)} %bitcast.15, bf16[72,4096]{1,0:T(8,128)(2,1)} %bitcast.16, bf16[72,4096]{1,0:T(8,128)(2,1)} %bitcast.17, f32[1,4096]{1,0:T(1,128)} %gain_ref.1, s32[72,4]{1,0:T(8,128)} %bitcast.20, f32[72,4]{1,0:T(8,128)} %bitcast.21, ...), custom_call_target="tpu_custom_call" | custom-call | tf_op jit(solution)/shard_map/pallas_call | solution.py:609
  166.3 1.9 %copy.19 = bf16[1,72,4096]{2,1,0:T(8,128)(2,1)} copy(bf16[1,72,4096]{2,1,0:T(8,128)(2,1)} %bitcast.19) | data formatting | bytes 1179648
  168.2 1.9 %copy.20 = bf16[1,72,4096]{2,1,0:T(8,128)(2,1)} copy(bf16[1,72,4096]{2,1,0:T(8,128)(2,1)} %bitcast.18) | data formatting | bytes 1179648
